TPU v7x, 256 devices: a whole 4x4x8 slice. The times are simulated.
256 devices in a mesh: grp: 8 (over z_lo, x), dev: 32 (over z_hi, y, core).
Axes of the slice: x: 4, y: 4, z: 8 (z_hi: 4, z_lo: 2; z = z_hi * 2 + z_lo), core: 2. Of those that a mesh axis runs over, the one named last changes fastest.
Arguments:
- pair_ft: bfloat16 [8192, 2, 4096], P('dev', None, 'grp'), may hold values from -6 to 6
- aux_ft: bfloat16 [4096, 2, 4096], P('dev', None, 'grp'), may hold values from -0.0625 to 0.0625
- coul_weight: float32 [4096], P('grp'), may hold values from 0.2 to 5
- aux_basis: bfloat16 [128, 4096], replicated, may hold values from -0.5 to 0.5
- aux_decay: float32 [4096], replicated, may hold values from 0.05 to 1
- image_dist: float32 [125], replicated, may hold values from 0 to 3
- image_phase: float32 [125], replicated, may hold values from -3.140625 to 3.140625
- item_pair: bfloat16 [4096, 128, 128], P(('grp', 'dev')), may hold values from -4 to 4
- item_image: int32 [4096], P(('grp', 'dev')), may hold values from 0 to 124
- item_sub: int32 [4096], P(('grp', 'dev')), may hold values from 0 to 1
- item_count: int32 [256], P(('grp', 'dev')), may hold values from 0 to 16, as said below
Outputs:
- j3c: bfloat16 [4096, 2, 8192], P('grp', None, 'dev')
Inputs may be any that keep to these rules, and one draw needn't show every extreme that they name: `item_count`: in every index of dev one of the 8 devices holds exactly 16 live slots. The counts of the 8 devices that share an index of dev sum to at most 72, and in every draw some index of dev reaches 72.
All inputs are finite; a program needn't handle non-finite values.
Results may differ from a plain program's by a relative error of at most 0.0047.
Values may be sent and summed in bfloat16 or wider, within the bound.
A program may use at most 64 MiB of HBM per device.

v0:
```python
import math

import jax
import jax.numpy as jnp
from jax import lax
from jax.sharding import PartitionSpec as P


def stacked_pairs(weighted):
    real_part = weighted[:, 0, :].T
    imag_part = weighted[:, 1, :].T
    real_cols = jnp.concatenate([real_part, imag_part], axis=0)
    imag_cols = jnp.concatenate([imag_part, -real_part], axis=0)
    return jnp.concatenate([real_cols, imag_cols], axis=1)


def short_range(
    aux_basis,
    aux_decay,
    image_dist,
    image_phase,
    first_row,
    row_count,
    blocks,
    images,
    sub_ids,
    usable,
    sub_count,
):
    basis_cols = lax.dynamic_slice_in_dim(aux_basis, first_row, row_count, 1)
    decay_rows = lax.dynamic_slice_in_dim(aux_decay, first_row, row_count, 0)
    products = jnp.einsum("kp,ikr->pir", basis_cols, blocks, preferred_element_type=jnp.float32)
    lookup = (images[:, None] == jnp.arange(image_dist.shape[0], dtype=jnp.int32)[None, :]).astype(
        jnp.float32
    )
    distance = jnp.dot(lookup, image_dist, precision=lax.Precision.HIGHEST)
    phase_value = jnp.dot(lookup, image_phase, precision=lax.Precision.HIGHEST)
    damping = jnp.exp(-decay_rows[:, None] * distance[None, :])
    factors = jnp.stack([jnp.cos(phase_value) * usable, jnp.sin(phase_value) * usable], axis=0)
    weights = damping[:, None, :] * factors[None, :, :]
    placing = (sub_ids[:, None] == jnp.arange(sub_count, dtype=jnp.int32)[None, :]).astype(
        jnp.float32
    )
    placed = jnp.einsum(
        "pir,pci,is->pcsr", products, weights, placing, precision=lax.Precision.HIGHEST
    )
    return placed.reshape(row_count, 2, sub_count * products.shape[2])


def body(
    pair_ft,
    aux_ft,
    coul_weight,
    aux_basis,
    aux_decay,
    image_dist,
    image_phase,
    item_pair,
    item_image,
    item_sub,
    item_count,
):
    group_count = lax.axis_size("grp")
    member_count = lax.axis_size("dev")
    capacity = item_image.shape[0]
    local_rows = pair_ft.shape[0]
    sub_rows = item_pair.shape[2]
    sub_count = local_rows // sub_rows
    aux_share = aux_ft.shape[0] * member_count // group_count
    weighted = (pair_ft.astype(jnp.float32) * coul_weight[None, None, :]).astype(jnp.bfloat16)

    def make_term(factors, factor_offset, pair_matrix, blocks, images, sub_ids, usable):

        def term_rows(first_row, row_count):
            block_rows = math.gcd(row_count, 512)

            def one_block(block_index):
                block_start = block_index * block_rows
                local_factors = lax.dynamic_slice_in_dim(
                    factors, block_start - factor_offset, block_rows, 0
                )
                factor_rows = local_factors.reshape(block_rows, -1)
                long_part = jnp.dot(factor_rows, pair_matrix, preferred_element_type=jnp.float32)
                long_part = long_part.reshape(block_rows, 2, local_rows)
                return long_part + short_range(
                    aux_basis,
                    aux_decay,
                    image_dist,
                    image_phase,
                    block_start,
                    block_rows,
                    blocks,
                    images,
                    sub_ids,
                    usable,
                    sub_count,
                )

            pieces = lax.map(one_block, jnp.arange(row_count // block_rows, dtype=jnp.int32))
            return pieces.reshape(row_count, 2, local_rows)

        return term_rows

    gathered = lax.all_gather(aux_ft, "dev", axis=0, tiled=True)
    blocks = item_pair
    images = item_image
    sub_ids = item_sub
    usable = jnp.arange(capacity, dtype=jnp.int32) < item_count[0]
    term_rows = make_term(
        gathered, 0, stacked_pairs(weighted), blocks, images, sub_ids, usable.astype(jnp.float32)
    )
    summed = lax.psum_scatter(
        term_rows(jnp.int32(0), aux_share * lax.axis_size("grp")),
        "grp",
        scatter_dimension=0,
        tiled=True,
    )
    return summed.astype(jnp.bfloat16)


def solution(mesh):
    return jax.shard_map(
        body,
        mesh=mesh,
        in_specs=(
            P("dev", None, "grp"),
            P("dev", None, "grp"),
            P("grp"),
            P(),
            P(),
            P(),
            P(),
            P(("grp", "dev"), None, None),
            P(("grp", "dev")),
            P(("grp", "dev")),
            P(("grp", "dev")),
        ),
        out_specs=P("grp", None, "dev"),
        check_vma=False,
    )
```

profile of v0, /device:TPU:32, one launch (start us, length us, event | category | flops | bytes accessed | tf_op | source)
XLA Modules:
  0.0 431.6 jit_solution(11790446058027590612)
XLA Ops:
  7.9 1.3 dynamic-slice
  9.8 0.9 fusion.14
  11.5 1.1 multiply_convert_fusion
  12.8 1.1 maximum_maximum_fusion
  13.8 76.6 %all-gather.2.cloned.1.call-done = bf16[4096,2,512]{2,1,0:T(2,128)(2,1)} async-done(((bf16[128,2,512]{2,1,0:T(2,128)(2,1)}), bf16[4096,2,512]{2,1,0:T(2,128)(2,1)}) %all-gather.2.cloned.1.call-update) | async-done | bytes 8388624 | tf_op jit(solution)/shard_map/all_gather | solution.py:104
  90.5 161.8 %while.14 = (s32[]{:T(128)}, f32[8,512,2,256]{3,2,1,0:T(2,128)}, s32[8]{0:T(128)S(1)}, bf16[4096,2,512]{2,1,0:T(2,128)(2,1)}, bf16[1024,512]{0,1:T(8,128)(2,1)},...) while((s32[]{:T(128)}, f32[8,512,2,256]{3,2,1,0:T(2,128)}, ...), condition=%wide.region_1.2_spmd, body=%wide.region_0.1_spmd.sunk | while | flops 855958080 | bytes 25042132 | solution.py:99
  92.9 1.8 convolution_bitcast_fusion.4
  94.7 8.0 %fusion.38 = f32[512,2,2,128]{3,1,2,0:T(2,128)S(1)} fusion(f32[512,16,128,1]{2,0,1,3:T(8,128)S(1)} %convolution_bitcast_fusion.4, f32[16,512,2]{0,2,1:T(2,128)S(1)} %multiply_bitcast_fusion.2, f32[16,2]{0,1:T(2,128)S(1)} %compare_convert_fusion.2), kind=kOutput, calls=%fused_computation.3.clone.1 | convolution fusion | flops 50364416 | bytes 5308544 | tf_op jit(solution)/shard_map/while/body/eval_jaxpr/pir,pci,is->pcsr/dot_general | solution.py:44
  104.2 2.0 constant_dynamic-slice_fusion.2
  106.9 2.0 fusion.39
  108.9 1.9 copy_dynamic-update-slice_fusion.2
  113.1 1.8 convolution_bitcast_fusion.4
  115.0 8.0 %fusion.38 = f32[512,2,2,128]{3,1,2,0:T(2,128)S(1)} fusion(f32[512,16,128,1]{2,0,1,3:T(8,128)S(1)} %convolution_bitcast_fusion.4, f32[16,512,2]{0,2,1:T(2,128)S(1)} %multiply_bitcast_fusion.2, f32[16,2]{0,1:T(2,128)S(1)} %compare_convert_fusion.2), kind=kOutput, calls=%fused_computation.3.clone.1 | convolution fusion | flops 50364416 | bytes 5308544 | tf_op jit(solution)/shard_map/while/body/eval_jaxpr/pir,pci,is->pcsr/dot_general | solution.py:44
  124.4 2.0 constant_dynamic-slice_fusion.2
  127.2 2.0 fusion.39
  129.1 1.8 copy_dynamic-update-slice_fusion.2
  133.3 1.8 convolution_bitcast_fusion.4
  135.2 8.0 %fusion.38 = f32[512,2,2,128]{3,1,2,0:T(2,128)S(1)} fusion(f32[512,16,128,1]{2,0,1,3:T(8,128)S(1)} %convolution_bitcast_fusion.4, f32[16,512,2]{0,2,1:T(2,128)S(1)} %multiply_bitcast_fusion.2, f32[16,2]{0,1:T(2,128)S(1)} %compare_convert_fusion.2), kind=kOutput, calls=%fused_computation.3.clone.1 | convolution fusion | flops 50364416 | bytes 5308544 | tf_op jit(solution)/shard_map/while/body/eval_jaxpr/pir,pci,is->pcsr/dot_general | solution.py:44
  144.6 2.0 constant_dynamic-slice_fusion.2
  147.4 2.0 fusion.39
  149.3 1.8 copy_dynamic-update-slice_fusion.2
  153.5 1.8 convolution_bitcast_fusion.4
  155.4 8.0 %fusion.38 = f32[512,2,2,128]{3,1,2,0:T(2,128)S(1)} fusion(f32[512,16,128,1]{2,0,1,3:T(8,128)S(1)} %convolution_bitcast_fusion.4, f32[16,512,2]{0,2,1:T(2,128)S(1)} %multiply_bitcast_fusion.2, f32[16,2]{0,1:T(2,128)S(1)} %compare_convert_fusion.2), kind=kOutput, calls=%fused_computation.3.clone.1 | convolution fusion | flops 50364416 | bytes 5308544 | tf_op jit(solution)/shard_map/while/body/eval_jaxpr/pir,pci,is->pcsr/dot_general | solution.py:44
  164.8 2.0 constant_dynamic-slice_fusion.2
  167.6 2.0 fusion.39
  169.5 1.8 copy_dynamic-update-slice_fusion.2
  173.8 1.8 convolution_bitcast_fusion.4
  175.6 8.0 %fusion.38 = f32[512,2,2,128]{3,1,2,0:T(2,128)S(1)} fusion(f32[512,16,128,1]{2,0,1,3:T(8,128)S(1)} %convolution_bitcast_fusion.4, f32[16,512,2]{0,2,1:T(2,128)S(1)} %multiply_bitcast_fusion.2, f32[16,2]{0,1:T(2,128)S(1)} %compare_convert_fusion.2), kind=kOutput, calls=%fused_computation.3.clone.1 | convolution fusion | flops 50364416 | bytes 5308544 | tf_op jit(solution)/shard_map/while/body/eval_jaxpr/pir,pci,is->pcsr/dot_general | solution.py:44
  185.1 2.0 constant_dynamic-slice_fusion.2
  187.8 2.0 fusion.39
  189.8 1.8 copy_dynamic-update-slice_fusion.2
  194.0 1.8 convolution_bitcast_fusion.4
  195.9 8.0 %fusion.38 = f32[512,2,2,128]{3,1,2,0:T(2,128)S(1)} fusion(f32[512,16,128,1]{2,0,1,3:T(8,128)S(1)} %convolution_bitcast_fusion.4, f32[16,512,2]{0,2,1:T(2,128)S(1)} %multiply_bitcast_fusion.2, f32[16,2]{0,1:T(2,128)S(1)} %compare_convert_fusion.2), kind=kOutput, calls=%fused_computation.3.clone.1 | convolution fusion | flops 50364416 | bytes 5308544 | tf_op jit(solution)/shard_map/while/body/eval_jaxpr/pir,pci,is->pcsr/dot_general | solution.py:44
  205.3 2.0 constant_dynamic-slice_fusion.2
  208.0 2.0 fusion.39
  210.0 1.8 copy_dynamic-update-slice_fusion.2
  214.2 1.9 convolution_bitcast_fusion.4
  216.1 8.0 %fusion.38 = f32[512,2,2,128]{3,1,2,0:T(2,128)S(1)} fusion(f32[512,16,128,1]{2,0,1,3:T(8,128)S(1)} %convolution_bitcast_fusion.4, f32[16,512,2]{0,2,1:T(2,128)S(1)} %multiply_bitcast_fusion.2, f32[16,2]{0,1:T(2,128)S(1)} %compare_convert_fusion.2), kind=kOutput, calls=%fused_computation.3.clone.1 | convolution fusion | flops 50364416 | bytes 5308544 | tf_op jit(solution)/shard_map/while/body/eval_jaxpr/pir,pci,is->pcsr/dot_general | solution.py:44
  225.5 2.0 constant_dynamic-slice_fusion.2
  228.3 2.0 fusion.39
  230.2 1.8 copy_dynamic-update-slice_fusion.2
  234.5 1.8 convolution_bitcast_fusion.4
  236.3 8.0 %fusion.38 = f32[512,2,2,128]{3,1,2,0:T(2,128)S(1)} fusion(f32[512,16,128,1]{2,0,1,3:T(8,128)S(1)} %convolution_bitcast_fusion.4, f32[16,512,2]{0,2,1:T(2,128)S(1)} %multiply_bitcast_fusion.2, f32[16,2]{0,1:T(2,128)S(1)} %compare_convert_fusion.2), kind=kOutput, calls=%fused_computation.3.clone.1 | convolution fusion | flops 50364416 | bytes 5308544 | tf_op jit(solution)/shard_map/while/body/eval_jaxpr/pir,pci,is->pcsr/dot_general | solution.py:44
  245.8 2.0 constant_dynamic-slice_fusion.2
  248.5 2.0 fusion.39
  250.5 1.8 copy_dynamic-update-slice_fusion.2
  252.3 170.3 %all-reduce.2 = bf16[4096,2,256]{2,1,0:T(2,128)(2,1)} all-reduce(f32[4096,2,256]{2,1,0:T(2,128)} %bitcast.74), channel_id=2, replica_groups=mesh['grp'=8,'dev'=32] {'grp'}, use_global_device_ids=true, to_apply=%region_2.3.clone | all-reduce | flops 2097152 | bytes 12582912
  422.5 2.2 dynamic-slice_convert_fusion
  (84 shorter events, 32.9 us)
Async XLA Ops:
  6.5 3.2 copy-start
  6.5 83.9 %copy-start.1 = (s32[16]{0:T(128)S(1)}, s32[16]{0:T(128)}, u32[]{:S(2)}) copy-start(s32[16]{0:T(128)} %param.22) | copy-start | bytes 196
  6.5 83.9 %all-gather.2.cloned.1.call-start = ((), (), s32[]{:S(2)}) async-start(), calls=%async_computation | async-start | bytes 8650752 | tf_op jit(solution)/shard_map/all_gather | solution.py:104
Sparse Core Ops, SparseCore 0:
  9.9 80.5 all-gather.1
where the time goes:
time: 435 us; the launch traced here: 432 us
  blocking collectives  170 us (39%)
  matrix products  96.5 us (22%)
  waiting for transfers between devices  77.3 us (18%)
  local copies, waits for them, and re-layouts  56.5 us (13%)
  between operations  14.7 us (3%)
  other arithmetic  10.5 us (2%)
  loops' own time  5.75 us (1%)
    unnamed x1, blocking collectives  170 us
    all_gather x1, waiting for transfers between devices, body(): gathered = lax.all_gather(aux_ft, 'dev', axis=0, tiled=True)  76.6 us
    dot_general x8, matrix products, short_range(): jnp.einsum('pir,pci,is->pcsr', products, weights, placing, precision=lax....  64.2 us
    dot_general x8, matrix products, one_block(): jnp.dot(factor_rows, pair_matrix, preferred_element_type=jnp.float32)  15.8 us
    dynamic_slice x8, local copies, waits for them, and re-layouts, one_block(): lax.dynamic_slice_in_dim(factors, block_start - factor_offset, block_rows...  15.6 us
    dot_general x8, matrix products, short_range(): jnp.einsum('kp,ikr->pir', basis_cols, blocks, preferred_element_type=jnp....  14.8 us
    dynamic_update_slice x8, local copies, waits for them, and re-layouts, term_rows(): lax.map(one_block, jnp.arange(row_count // block_rows, dtype=jnp.int32))  14.5 us
  transfers between devices with their start and end apart: 1, of which 1 were waited for; matrix products, arithmetic and copies ran while one was open for 1% of the time, Pallas kernels for 0%

commit v1 on v0

v1 whole, which is shorter than its diff:
```python
import jax
import jax.numpy as jnp
from jax import lax
from jax.experimental import pallas as pl
from jax.experimental.pallas import tpu as pltpu
from jax.sharding import PartitionSpec as P

MESH = pl.DeviceIdType.MESH
HALVES = 2
SIDE = 4
ORDER = ((0, 0), (0, 1), (1, 0), (2, 0), (1, 1), (2, 1), (3, 0), (3, 1))
STEP_OF = {entry: index for index, entry in enumerate(ORDER)}
STEPS = len(ORDER)


def offset_of(index):
    high = index // 2
    return 2 * high + (high + index) % 2


def wrap(value):
    return lax.rem(value + 8, 4)


def kernel(
    aux_ref,
    pair_ref,
    basis_ref,
    decay_ref,
    items_ref,
    dist_ref,
    phase_ref,
    image_ref,
    sub_ref,
    count_ref,
    out_ref,
    factors,
    total,
    ring_in,
    ring_out,
    pair_in,
    long_rhs,
    short_rhs,
    basis_rows,
    decay_rows,
    damped,
    scales,
    load_sem,
    factor_recv,
    z_send,
    z_relay,
    y_send,
    y_relay,
    core_send,
    ring_send,
    ring_recv,
    pair_recv,
):
    group, member = lax.axis_index("grp"), lax.axis_index("dev")
    z_low, x = lax.div(group, 4), lax.rem(group, 4)
    core, y, z = lax.rem(member, 2), lax.rem(lax.div(member, 2), 4), lax.div(member, 8)
    way = 1 - 2 * core
    piece = factors.shape[3]
    items = items_ref.shape[0]
    rank = items_ref.shape[1]
    columns = long_rhs.shape[0]
    side_rows = columns // 2
    half_k = pair_ref.shape[1] // 2

    def place(z_at, y_at, core_at):
        return (group, (z_at * 4 + y_at) * 2 + core_at)

    own = z * 4 + y
    for half in range(HALVES):
        pltpu.make_async_copy(
            aux_ref.at[pl.ds(half * piece, piece)], factors.at[half, own, core], load_sem.at[half]
        ).start()

    peers = (
        place(wrap(z + 1), y, core),
        place(wrap(z - 1), y, core),
        place(z, wrap(y + 1), core),
        place(z, wrap(y - 1), core),
        place(z, y, 1 - core),
        (z_low * 4 + wrap(x + 1), member),
        (z_low * 4 + wrap(x - 1), member),
        ((1 - z_low) * 4 + x, member),
    )
    barrier = pltpu.get_barrier_semaphore()
    for peer in peers:
        pl.semaphore_signal(barrier, inc=1, device_id=peer, device_id_type=MESH)
    pl.semaphore_wait(barrier, len(peers))

    def factor_copy(half, chip, core_at, target, send_sem):
        return pltpu.make_async_remote_copy(
            src_ref=factors.at[half, chip, core_at],
            dst_ref=factors.at[half, chip, core_at],
            send_sem=send_sem,
            recv_sem=factor_recv.at[half * 32 + chip * 2 + core_at],
            device_id=target,
            device_id_type=MESH,
        )

    def await_factor(half, chip, core_at):
        factor_copy(half, chip, core_at, peers[4], load_sem.at[0]).wait_recv()

    waits = []

    def send(half, chip, target, send_sem):
        copy = factor_copy(half, chip, core, target, send_sem)
        copy.start()
        waits.append(copy)

    def chip_at(z_step, y_step):
        return wrap(z + offset_of(z_step)) * 4 + wrap(y + y_step)

    def relay_column(step):
        z_step, half = ORDER[step]
        chip = chip_at(z_step, 0)
        if z_step == 0:
            pltpu.make_async_copy(
                aux_ref.at[pl.ds(half * piece, piece)], factors.at[half, own, core], load_sem.at[half]
            ).wait()
            send(half, chip, peers[0], z_send.at[half * 2])
            send(half, chip, peers[1], z_send.at[half * 2 + 1])
        else:
            await_factor(half, chip, core)
        send(half, chip, peers[2], y_send.at[step * 2])
        send(half, chip, peers[3], y_send.at[step * 2 + 1])
        if z_step == 1 or z_step == 2:
            onward = peers[1] if z_step == 1 else peers[0]

            @pl.when(core == 2 - z_step)
            def _():
                factor_copy(half, chip, core, onward, z_relay.at[half]).start()

        send(half, chip, peers[4], core_send.at[step * 4])

    def relay_row(step):
        z_step, half = ORDER[step]
        behind, ahead = chip_at(z_step, -way), chip_at(z_step, way)
        await_factor(half, behind, core)
        send(half, behind, place(z, wrap(y + way), core), y_relay.at[step])
        send(half, behind, peers[4], core_send.at[step * 4 + 1])
        await_factor(half, ahead, core)
        send(half, ahead, peers[4], core_send.at[step * 4 + 2])

    def relay_far(step):
        z_step, half = ORDER[step]
        far = chip_at(z_step, 2)
        await_factor(half, far, core)
        send(half, far, peers[4], core_send.at[step * 4 + 3])

    def prepare():
        long_rhs[0:side_rows, :] = pair_ref[...]
        long_rhs[side_rows:columns, 0:half_k] = pair_ref[:, half_k:]
        long_rhs[side_rows:columns, half_k:] = -pair_ref[:, 0:half_k]

        def transpose(index, carry):
            rows = pl.ds(pl.multiple_of(index * 128, 128), 128)
            basis_rows[rows, :] = basis_ref[:, rows].astype(jnp.float32).T
            decay_rows[rows, :] = jnp.broadcast_to(decay_ref[pl.ds(index, 1), :], (128, 128)).T
            return carry

        lax.fori_loop(0, basis_rows.shape[0] // 128, transpose, 0)

        slot = lax.broadcasted_iota(jnp.int32, (items, 128), 0)
        phases = jnp.zeros((items, 128), jnp.float32)
        first = jnp.zeros((items, 128), jnp.float32)
        second = jnp.zeros((items, 128), jnp.float32)
        for index in range(items):
            alive = jnp.where(index < count_ref[0], 1.0, 0.0)
            to_second = sub_ref[index].astype(jnp.float32)
            phases = jnp.where(slot == index, phase_ref[image_ref[index]], phases)
            first = jnp.where(slot == index, alive * (1.0 - to_second), first)
            second = jnp.where(slot == index, alive * to_second, second)
        cosine, sine = jnp.cos(phases), jnp.sin(phases)
        scales[0] = cosine * first
        scales[1] = cosine * second
        scales[2] = sine * first
        scales[3] = sine * second

        def place_item(index, carry):
            block = items_ref[index].astype(jnp.float32)
            rows = pl.ds(pl.multiple_of(index * rank, rank), rank)
            for part in range(4):
                short_rhs[rows, part * 128 : (part + 1) * 128] = (
                    block * scales[part, pl.ds(index, 1), :]
                ).astype(jnp.bfloat16)
            return carry

        lax.fori_loop(0, items, place_item, 0)

    def short_range(z_step):
        def one(y_step, carry):
            chip = chip_at(z_step, offset_of(y_step))
            rows = pl.ds(pl.multiple_of(chip * 4 * piece, 4 * piece), 4 * piece)
            for index in range(items):
                weight = jnp.exp(decay_rows[rows, :] * (-dist_ref[image_ref[index]]))
                damped[:, index * rank : (index + 1) * rank] = (weight * basis_rows[rows, :]).astype(
                    jnp.bfloat16
                )
            product = jnp.dot(damped[...], short_rhs[...], preferred_element_type=jnp.float32)
            for half in range(HALVES):
                for core_at in range(2):
                    start = (core_at * HALVES + half) * piece
                    total[STEP_OF[z_step, half] * 4 + y_step, core_at * piece : (core_at + 1) * piece, :] = (
                        product[start : start + piece]
                    )
            return carry

        lax.fori_loop(0, SIDE, one, 0)

    def long_range(step):
        z_step, half = ORDER[step]

        def one(y_step, carry):
            chip = chip_at(z_step, offset_of(y_step))
            await_factor(half, chip, 1 - core)
            rows = factors[half, chip].reshape(2 * piece, 2 * half_k)
            total[step * 4 + y_step] += lax.dot_general(
                rows, long_rhs[...], (((1,), (1,)), ((), ())), preferred_element_type=jnp.float32
            )
            return carry

        lax.fori_loop(0, SIDE, one, 0)

    def roles(step, y_step):
        z_step, _ = ORDER[step]
        z_at = wrap(z + offset_of(z_step))
        y_at = wrap(y + offset_of(y_step))
        x_at = lax.rem(z_at, 2) * 2 + lax.div(y_at, 2)
        hop = wrap((x - x_at) * way - 1)
        return hop, lax.div(z_at, 2) == z_low, lax.rem(y_at, 2)

    def ring_copy(block):
        return pltpu.make_async_remote_copy(
            src_ref=ring_out.at[block],
            dst_ref=ring_in.at[block],
            send_sem=ring_send.at[block],
            recv_sem=ring_recv.at[block],
            device_id=(z_low * 4 + wrap(x + way), member),
            device_id_type=MESH,
        )

    def pair_copy(block):
        return pltpu.make_async_remote_copy(
            src_ref=ring_out.at[block],
            dst_ref=pair_in.at[block],
            send_sem=ring_send.at[block],
            recv_sem=pair_recv.at[block],
            device_id=peers[7],
            device_id_type=MESH,
        )

    def reduce_hops(step):
        def one(y_step, carry):
            for lag in range(5):
                at = step - lag
                if at < 0 or at >= STEPS:
                    continue
                block = at * 4 + y_step
                hop, keeps, odd_y = roles(at, y_step)
                if lag == 0:

                    @pl.when(hop == 0)
                    def _():
                        ring_out[block] = total[block].astype(jnp.bfloat16)
                        ring_copy(block).start()

                elif lag < 3:

                    @pl.when(hop == lag)
                    def _():
                        ring_copy(block).wait_recv()
                        ring_out[block] = (total[block] + ring_in[block].astype(jnp.float32)).astype(
                            jnp.bfloat16
                        )
                        ring_copy(block).start()

                elif lag == 3:

                    @pl.when((hop == 3) & keeps)
                    def _():
                        ring_copy(block).wait_recv()
                        total[block] += ring_in[block].astype(jnp.float32)

                    @pl.when((hop == 3) & jnp.logical_not(keeps))
                    def _():
                        ring_copy(block).wait_recv()
                        ring_out[block] = (total[block] + ring_in[block].astype(jnp.float32)).astype(
                            jnp.bfloat16
                        )
                        pair_copy(block).start()

                else:
                    _, half = ORDER[at]

                    @pl.when((hop == 3) & keeps)
                    def _():
                        pair_copy(block).wait_recv()
                        done = (total[block] + pair_in[block].astype(jnp.float32)).astype(jnp.bfloat16)
                        for core_at in range(2):
                            start = odd_y * (4 * piece) + (core_at * HALVES + half) * piece
                            out_ref[pl.ds(pl.multiple_of(start, piece), piece), :] = done[
                                core_at * piece : (core_at + 1) * piece
                            ]

            return carry

        lax.fori_loop(0, SIDE, one, 0)

    relay_column(0)
    relay_column(1)
    prepare()
    short_range(0)
    relay_row(0)
    relay_row(1)
    relay_column(2)
    relay_column(3)
    short_range(1)
    for step in range(STEPS + 4):
        if step + 3 < STEPS and step > 0:
            relay_column(step + 3)
        if step + 1 < STEPS and step > 0:
            relay_row(step + 1)
        if step < STEPS:
            relay_far(step)
            long_range(step)
        reduce_hops(step)
        if step < 2:
            short_range(step + 2)

    for copy in waits:
        copy.wait_send()
    for z_step in (1, 2):
        for half in range(HALVES):

            @pl.when(core == 2 - z_step)
            def _():
                factor_copy(half, own, core, peers[0], z_relay.at[half]).wait_send()

    for step in range(STEPS):

        def drain(y_step, carry):
            hop, keeps, _ = roles(step, y_step)

            @pl.when((hop < 3) | jnp.logical_not(keeps))
            def _():
                ring_copy(step * 4 + y_step).wait_send()

            return carry

        lax.fori_loop(0, SIDE, drain, 0)


def body(
    pair_ft,
    aux_ft,
    coul_weight,
    aux_basis,
    aux_decay,
    image_dist,
    image_phase,
    item_pair,
    item_image,
    item_sub,
    item_count,
):
    rows, _, depth = pair_ft.shape
    share = aux_ft.shape[0]
    aux_rows = aux_basis.shape[1]
    capacity, rank, _ = item_pair.shape
    columns = 2 * rows
    piece = share // HALVES
    weighted = (pair_ft.astype(jnp.float32) * coul_weight[None, None, :]).astype(jnp.bfloat16)
    pair_rows = weighted.reshape(rows, 2 * depth)
    factors = aux_ft.reshape(share, 2 * depth)
    blocks = STEPS * SIDE
    vmem = pl.BlockSpec(memory_space=pltpu.VMEM)
    smem = pl.BlockSpec(memory_space=pltpu.SMEM)
    dma = pltpu.SemaphoreType.DMA
    result = pl.pallas_call(
        kernel,
        out_shape=jax.ShapeDtypeStruct((aux_rows // lax.axis_size("grp"), columns), jnp.bfloat16),
        in_specs=[pl.BlockSpec(memory_space=pl.ANY)] + [vmem] * 4 + [smem] * 5,
        out_specs=vmem,
        scratch_shapes=[
            pltpu.VMEM((HALVES, 16, 2, piece, 2 * depth), jnp.bfloat16),
            pltpu.VMEM((blocks, 2 * piece, columns), jnp.float32),
            pltpu.VMEM((blocks, 2 * piece, columns), jnp.bfloat16),
            pltpu.VMEM((blocks, 2 * piece, columns), jnp.bfloat16),
            pltpu.VMEM((blocks, 2 * piece, columns), jnp.bfloat16),
            pltpu.VMEM((columns, 2 * depth), jnp.bfloat16),
            pltpu.VMEM((capacity * rank, columns), jnp.bfloat16),
            pltpu.VMEM((aux_rows, rank), jnp.float32),
            pltpu.VMEM((aux_rows, rank), jnp.float32),
            pltpu.VMEM((2 * share, capacity * rank), jnp.bfloat16),
            pltpu.VMEM((4, capacity, 128), jnp.float32),
            dma((HALVES,)),
            dma((HALVES * 32,)),
            dma((HALVES * 2,)),
            dma((HALVES,)),
            dma((STEPS * 2,)),
            dma((STEPS,)),
            dma((STEPS * 4,)),
            dma((blocks,)),
            dma((blocks,)),
            dma((blocks,)),
        ],
        compiler_params=pltpu.CompilerParams(
            collective_id=0, has_side_effects=True, vmem_limit_bytes=60 * 2**20
        ),
    )(
        factors,
        pair_rows,
        aux_basis,
        aux_decay.reshape(aux_rows // 128, 128),
        item_pair,
        image_dist,
        image_phase,
        item_image,
        item_sub,
        item_count,
    )
    return result.reshape(result.shape[0], 2, rows)


def solution(mesh):
    return jax.shard_map(
        body,
        mesh=mesh,
        in_specs=(
            P("dev", None, "grp"),
            P("dev", None, "grp"),
            P("grp"),
            P(),
            P(),
            P(),
            P(),
            P(("grp", "dev"), None, None),
            P(("grp", "dev")),
            P(("grp", "dev")),
            P(("grp", "dev")),
        ),
        out_specs=P("grp", None, "dev"),
        check_vma=False,
    )
```

time: 435 us -> 99.3 us (0.23)
  blocking collectives: 170 us -> 0 us
  matrix products: 96.5 us -> 0 us
  Pallas kernels: 0 us -> 93.4 us
  waiting for transfers between devices: 77.3 us -> 0 us
  local copies, waits for them, and re-layouts: 56.5 us -> 4.52 us
  between operations: 14.7 us -> 0.73 us
  other arithmetic: 10.5 us -> 0.41 us
  loops' own time: 5.75 us -> 0 us
    unnamed x1 -> x0, blocking collectives: 170 us -> none
    dot_general x26 -> x0, matrix products: 96.5 us -> none  [the longest x8 64.2 us: short_range(): jnp.einsum('pir,pci,is->pcsr', products, weights, placing, precision=lax....]
    pallas_call x0 -> x1, Pallas kernels: none -> 93.4 us  [body(): pl.pallas_call(kernel, out_shape=jax.ShapeDtypeStruct((aux_rows // lax.ax...]
    all_gather x1 -> x0, waiting for transfers between devices: 76.6 us -> none  [body(): gathered = lax.all_gather(aux_ft, 'dev', axis=0, tiled=True)]
    dynamic_slice x16 -> x0, local copies, waits for them, and re-layouts: 20.4 us -> none  [the longest x8 15.6 us: one_block(): lax.dynamic_slice_in_dim(factors, block_start - factor_offset, block_rows...]
    dynamic_update_slice x8 -> x0, local copies, waits for them, and re-layouts: 14.5 us -> none  [term_rows(): lax.map(one_block, jnp.arange(row_count // block_rows, dtype=jnp.int32))]
    reshape x16 -> x1, local copies, waits for them, and re-layouts: 12.8 us -> 1.96 us  [body(): return result.reshape(result.shape[0], 2, rows)]
    neg x9 -> x0, other arithmetic: 6.14 us -> none  [the longest x8 6.12 us: short_range(): damping = jnp.exp(-decay_rows[:, None] * distance[None, :])]
  transfers between devices with their start and end apart: 1 -> 0, of which waited for: 1 -> 0; matrix products, arithmetic and copies ran while one was open for 1% -> 0% of each run, Pallas kernels for 0% -> 0%
where the time goes in v1:
time: 99.3 us; the launch traced here: 99.1 us
  Pallas kernels  93.4 us (94%)
  local copies, waits for them, and re-layouts  4.52 us (5%)
    pallas_call x1, Pallas kernels, body(): pl.pallas_call(kernel, out_shape=jax.ShapeDtypeStruct((aux_rows // lax.ax...  93.4 us
    unnamed x6, local copies, waits for them, and re-layouts  2.56 us

profile of v1, /device:TPU:32, one launch (start us, length us, event | category | flops | bytes accessed | tf_op | source)
XLA Modules:
  0.0 99.1 jit_solution(16339838421117652607)
XLA Ops:
  0.0 0.0 copy-start
  0.7 0.0 copy-start.1
  0.7 1.7 %copy.12 = bf16[16,8,2,512]{3,1,2,0:T(8,128)(2,1)} copy(bf16[16,8,2,512]{3,2,1,0:T(2,128)(2,1)} %bitcast.8) | data formatting | bytes 524288
  2.4 0.0 copy-done
  2.4 0.0 copy-done.1
  2.4 0.4 multiply_convert_fusion
  2.8 0.9 copy.13
  3.7 93.4 %shard_map.109 = bf16[512,512]{1,0:T(8,128)(2,1)} custom-call(bf16[128,1024]{1,0:T(8,128)(2,1)} %bitcast.7, bf16[256,1024]{1,0:T(8,128)(2,1)} %bitcast.6, bf16[128,4096]{1,0:T(8,128)(2,1)} %basis_ref.1, f32[32,128]{1,0:T(8,128)} %bitcast.9, bf16[16,128,128]{2,1,0:T(8,128)(2,1)} %items_ref.1, f32[125]{0:T(128)} %dist_ref.1, f32[125]{0:T(128)} %phase_ref.1, ...), custom_call_target="tpu_custom_call" | custom-call | tf_op jit(solution)/shard_map/pallas_call | solution.py:383
  97.1 2.0 %reshape.16 = bf16[512,2,256]{2,1,0:T(2,128)(2,1)} reshape(bf16[512,512]{1,0:T(8,128)(2,1)} %shard_map.109) | data formatting | bytes 1048576 | tf_op jit(solution)/shard_map/reshape | solution.py:426
Async XLA Ops:
  0.0 2.4 %copy-start = (bf16[256,2,512]{2,1,0:T(2,128)(2,1)S(1)}, bf16[256,2,512]{2,1,0:T(2,128)(2,1)}, u32[]{:S(2)}) copy-start(bf16[256,2,512]{2,1,0:T(2,128)(2,1)} %param.11) | copy-start | bytes 1572868
  0.7 1.7 %copy-start.1 = (f32[512]{0:T(512)S(1)}, f32[512]{0:T(512)}, u32[]{:S(2)}) copy-start(f32[512]{0:T(512)} %param.13) | copy-start | bytes 6148

commit v2 on v1

v2 whole, which is shorter than its diff:
```python
import jax
import jax.numpy as jnp
from jax import lax
from jax.experimental import pallas as pl
from jax.experimental.pallas import tpu as pltpu
from jax.sharding import PartitionSpec as P

MESH = pl.DeviceIdType.MESH
HALVES = 2
SIDE = 4
STEPS = SIDE * HALVES
QUADS = ((0, 0, 0), (0, 2, 0), (0, 0, 1), (0, 2, 1), (2, 0, 0), (2, 2, 0), (2, 0, 1), (2, 2, 1))


def offset_of(index):
    high = index // 2
    return 2 * high + (high + index) % 2


def step_of(z_step, half):
    return z_step * HALVES + half


def wrap(value):
    return lax.rem(value + 8, 4)


def kernel(
    aux_ref,
    pair_ref,
    basis_ref,
    decay_ref,
    items_ref,
    dist_ref,
    phase_ref,
    image_ref,
    sub_ref,
    count_ref,
    out_ref,
    factors,
    total,
    chain_in,
    side_in,
    pair_in,
    reduce_out,
    long_lhs,
    short_lhs,
    basis_cols,
    damping,
    damped,
    scales,
    load_sem,
    factor_recv,
    z_send,
    z_relay,
    y_send,
    y_relay,
    core_send,
    reduce_send,
    chain_recv,
    side_recv,
    pair_recv,
):
    group, member = lax.axis_index("grp"), lax.axis_index("dev")
    z_low, x = lax.div(group, 4), lax.rem(group, 4)
    core, y, z = lax.rem(member, 2), lax.rem(lax.div(member, 2), 4), lax.div(member, 8)
    way = 1 - 2 * core
    piece = factors.shape[3]
    items = items_ref.shape[0]
    rank = items_ref.shape[1]
    columns = long_lhs.shape[0]
    side_rows = columns // 2
    depth = pair_ref.shape[1]
    half_k = depth // 2

    def place(z_at, y_at, core_at):
        return (group, (z_at * 4 + y_at) * 2 + core_at)

    def own_copy(half):
        return pltpu.make_async_copy(
            aux_ref.at[pl.ds(half * piece, piece)],
            factors.at[step_of(0, half), 0, core],
            load_sem.at[half],
        )

    for half in range(HALVES):
        own_copy(half).start()

    sibling = place(z, y, 1 - core)
    z_peers = (place(wrap(z + 1), y, core), place(wrap(z - 1), y, core))
    turn = 2 * lax.rem(y, 2) - 1
    y_peers = (place(z, wrap(y + turn), core), place(z, wrap(y - turn), core))
    y_ahead = place(z, wrap(y + way), core)
    x_down = (z_low * 4 + wrap(x - way), member)
    x_up = (z_low * 4 + wrap(x + way), member)
    z_pair = ((1 - z_low) * 4 + x, member)
    seen_as = (2, 1)

    peers = z_peers + y_peers + (sibling, x_down, x_up, z_pair)
    barrier = pltpu.get_barrier_semaphore()
    for peer in peers:
        pl.semaphore_signal(barrier, inc=1, device_id=peer, device_id_type=MESH)
    pl.semaphore_wait(barrier, len(peers))

    waits = []

    def factor_copy(source, sink, target, send_sem):
        step, row = sink
        return pltpu.make_async_remote_copy(
            src_ref=factors.at[source[0], source[1], core],
            dst_ref=factors.at[step, row, core],
            send_sem=send_sem,
            recv_sem=factor_recv.at[(step * 4 + row) * 2 + core],
            device_id=target,
            device_id_type=MESH,
        )

    def send(source, sink, target, send_sem):
        copy = factor_copy(source, sink, target, send_sem)
        copy.start()
        waits.append(copy)

    def await_factor(step, row, core_at):
        pltpu.make_async_remote_copy(
            src_ref=factors.at[step, row, core_at],
            dst_ref=factors.at[step, row, core_at],
            send_sem=load_sem.at[0],
            recv_sem=factor_recv.at[(step * 4 + row) * 2 + core_at],
            device_id=sibling,
            device_id_type=MESH,
        ).wait_recv()

    def relay_copy(z_step, half):
        step = step_of(z_step, half)
        return factor_copy(
            (step, 0), (step_of(3, half), 0), z_peers[2 - z_step], z_relay.at[half]
        )

    def send_column(z_step, half):
        step = step_of(z_step, half)
        if z_step == 0:
            own_copy(half).wait()
            for index, target in enumerate(z_peers):
                sink = (step_of(seen_as[index], half), 0)
                send((step, 0), sink, target, z_send.at[half * 2 + index])
        else:
            await_factor(step, 0, core)
            if z_step < 3:

                @pl.when(core == 2 - z_step)
                def _():
                    relay_copy(z_step, half).start()

        for index, target in enumerate(y_peers):
            send((step, 0), (step, index + 1), target, y_send.at[step * 2 + index])
        send((step, 0), (step, 0), sibling, core_send.at[step * 4])

    def send_rows(z_step, half):
        step = step_of(z_step, half)
        behind = 1 + lax.rem(core + y, 2)
        await_factor(step, behind, core)
        send((step, behind), (step, 3), y_ahead, y_relay.at[step])
        send((step, behind), (step, behind), sibling, core_send.at[step * 4 + 1])
        await_factor(step, 3 - behind, core)
        send((step, 3 - behind), (step, 3 - behind), sibling, core_send.at[step * 4 + 2])

    def send_far(z_step, half):
        step = step_of(z_step, half)
        await_factor(step, 3, core)
        send((step, 3), (step, 3), sibling, core_send.at[step * 4 + 3])

    def prepare():
        long_lhs[0:side_rows, :] = pair_ref[...]
        long_lhs[side_rows:columns, 0:half_k] = pair_ref[:, half_k:]
        long_lhs[side_rows:columns, half_k:] = -pair_ref[:, 0:half_k]

        slot = lax.broadcasted_iota(jnp.int32, (items, 128), 0)
        phases = jnp.zeros((items, 128), jnp.float32)
        reach = jnp.zeros((items, 128), jnp.float32)
        first = jnp.zeros((items, 128), jnp.float32)
        second = jnp.zeros((items, 128), jnp.float32)
        for index in range(items):
            alive = jnp.where(index < count_ref[0], 1.0, 0.0)
            to_second = sub_ref[index].astype(jnp.float32)
            phases = jnp.where(slot == index, phase_ref[image_ref[index]], phases)
            reach = jnp.where(slot == index, -dist_ref[image_ref[index]], reach)
            first = jnp.where(slot == index, alive * (1.0 - to_second), first)
            second = jnp.where(slot == index, alive * to_second, second)
        cosine, sine = jnp.cos(phases), jnp.sin(phases)
        scales[0] = cosine * first
        scales[1] = cosine * second
        scales[2] = sine * first
        scales[3] = sine * second

        def place_item(index, carry):
            block = items_ref[index].astype(jnp.float32).T
            at = pl.ds(pl.multiple_of(index * rank, rank), rank)
            for part in range(4):
                short_lhs[part * 128 : (part + 1) * 128, at] = (
                    block * scales[part, pl.ds(index, 1), :]
                ).astype(jnp.bfloat16)
            return carry

        lax.fori_loop(0, items, place_item, 0)

        def by_halves(left, right):
            low = lax.broadcasted_iota(jnp.int32, left.shape, 1) < piece
            return (
                jnp.where(low, left, pltpu.roll(right, piece, 1)),
                jnp.where(low, pltpu.roll(left, piece, 1), right),
            )

        def arrange(chip, carry):
            at = pl.multiple_of(chip * 256, 256)
            left, right = pl.ds(at, 128), pl.ds(at + 128, 128)
            basis_cols[:, left], basis_cols[:, right] = by_halves(
                basis_ref[:, left].astype(jnp.float32), basis_ref[:, right].astype(jnp.float32)
            )
            damping[:, left], damping[:, right] = by_halves(
                jnp.exp(reach * decay_ref[pl.ds(chip * 2, 1), :]),
                jnp.exp(reach * decay_ref[pl.ds(chip * 2 + 1, 1), :]),
            )
            return carry

        lax.fori_loop(0, basis_cols.shape[1] // 256, arrange, 0)

    def short_range(z_step):
        def one(y_step, carry):
            chip = wrap(z + offset_of(z_step)) * 4 + wrap(y + turn * offset_of(y_step))
            at = pl.ds(pl.multiple_of(chip * 256, 256), 256)
            for index in range(items):
                damped[index * rank : (index + 1) * rank, :] = (
                    basis_cols[:, at] * damping[index : index + 1, at]
                ).astype(jnp.bfloat16)
            product = jnp.dot(short_lhs[...], damped[...], preferred_element_type=jnp.float32)
            for half in range(HALVES):
                total[step_of(z_step, half) * 4 + y_step] = product[:, half * 128 : (half + 1) * 128]
            return carry

        lax.fori_loop(0, SIDE, one, 0)

    def roles(z_step, row):
        z_at = wrap(z + offset_of(z_step))
        y_at = wrap(y + turn * offset_of(row))
        x_at = lax.rem(z_at, 2) * 2 + lax.div(y_at, 2)
        role = wrap((x - x_at) * way)
        return role, lax.div(z_at, 2) == z_low, lax.rem(y_at, 2)

    def reduce_copy(block, sink, recv_sem, target):
        return pltpu.make_async_remote_copy(
            src_ref=reduce_out.at[block],
            dst_ref=sink.at[block],
            send_sem=reduce_send.at[block],
            recv_sem=recv_sem.at[block],
            device_id=target,
            device_id_type=MESH,
        )

    def chain_copy(block):
        return reduce_copy(block, chain_in, chain_recv, x_down)

    def side_copy(block):
        return reduce_copy(block, side_in, side_recv, x_up)

    def pair_copy(block):
        return reduce_copy(block, pair_in, pair_recv, z_pair)

    def long_range(quad):
        first_z, first_row, half = quad

        def one(pair, carry):
            z_step = first_z + pair
            step = step_of(z_step, half)
            for row in range(2):
                await_factor(step, first_row + row, 1 - core)
            rows = factors[step, first_row : first_row + 2].reshape(4 * piece, depth)
            product = lax.dot_general(
                long_lhs[...], rows, (((1,), (1,)), ((), ())), preferred_element_type=jnp.float32
            )
            for row in range(2):
                block = step * 4 + first_row + row
                total[block] += product[:, row * 128 : (row + 1) * 128]
                role, _, _ = roles(z_step, first_row + row)

                @pl.when(role >= 2)
                def _():
                    reduce_out[block] = total[block].astype(jnp.bfloat16)

                @pl.when(role == 2)
                def _():
                    chain_copy(block).start()

                @pl.when(role == 3)
                def _():
                    side_copy(block).start()

            return carry

        lax.fori_loop(0, 2, one, 0)

    def reduce_hop(quad, hop):
        first_z, first_row, half = quad

        def one(index, carry):
            z_step = first_z + index // 2
            row = first_row + index % 2
            block = step_of(z_step, half) * 4 + row
            role, keeps, odd_y = roles(z_step, row)
            if hop == 1:

                @pl.when(role == 1)
                def _():
                    chain_copy(block).wait_recv()
                    reduce_out[block] = (total[block] + chain_in[block].astype(jnp.float32)).astype(
                        jnp.bfloat16
                    )
                    chain_copy(block).start()

            elif hop == 2:

                @pl.when(role == 0)
                def _():
                    side_copy(block).wait_recv()
                    chain_copy(block).wait_recv()
                    total[block] += chain_in[block].astype(jnp.float32) + side_in[block].astype(
                        jnp.float32
                    )

                @pl.when((role == 0) & jnp.logical_not(keeps))
                def _():
                    reduce_out[block] = total[block].astype(jnp.bfloat16)
                    pair_copy(block).start()

            else:

                @pl.when((role == 0) & keeps)
                def _():
                    pair_copy(block).wait_recv()
                    done = (total[block] + pair_in[block].astype(jnp.float32)).T
                    for core_at in range(2):
                        start = odd_y * (4 * piece) + (core_at * HALVES + half) * piece
                        out_ref[pl.ds(pl.multiple_of(start, piece), piece), :] = done[
                            core_at * piece : (core_at + 1) * piece
                        ].astype(jnp.bfloat16)

            return carry

        lax.fori_loop(0, SIDE, one, 0)

    def advance(index):
        if index < len(QUADS):
            long_range(QUADS[index])
        for hop in (1, 2, 3):
            if 0 <= index - hop < len(QUADS):
                reduce_hop(QUADS[index - hop], hop)

    send_column(0, 0)
    send_column(0, 1)
    prepare()
    short_range(0)
    send_rows(0, 0)
    send_rows(0, 1)
    send_column(1, 0)
    send_column(2, 0)
    short_range(1)
    send_far(0, 0)
    send_rows(1, 0)
    send_far(0, 1)
    send_column(1, 1)
    advance(0)
    send_rows(2, 0)
    send_far(1, 0)
    send_column(3, 0)
    send_column(2, 1)
    advance(1)
    short_range(2)
    send_rows(1, 1)
    send_column(3, 1)
    advance(2)
    send_far(2, 0)
    send_far(1, 1)
    send_rows(3, 0)
    advance(3)
    short_range(3)
    send_rows(2, 1)
    advance(4)
    send_far(3, 0)
    send_rows(3, 1)
    advance(5)
    send_far(2, 1)
    advance(6)
    send_far(3, 1)
    for index in range(7, 11):
        advance(index)

    for copy in waits:
        copy.wait_send()
    for half in range(HALVES):
        relay_copy(1, half).wait_send()
    def drain(block, carry):
        role, keeps, _ = roles(block // (HALVES * SIDE), block % SIDE)

        @pl.when((role > 0) | jnp.logical_not(keeps))
        def _():
            chain_copy(block).wait_send()

        return carry

    lax.fori_loop(0, STEPS * SIDE, drain, 0)


def body(
    pair_ft,
    aux_ft,
    coul_weight,
    aux_basis,
    aux_decay,
    image_dist,
    image_phase,
    item_pair,
    item_image,
    item_sub,
    item_count,
):
    rows, _, depth = pair_ft.shape
    share = aux_ft.shape[0]
    aux_rows = aux_basis.shape[1]
    capacity, rank, _ = item_pair.shape
    columns = 2 * rows
    piece = share // HALVES
    weighted = (pair_ft.astype(jnp.float32) * coul_weight[None, None, :]).astype(jnp.bfloat16)
    pair_rows = weighted.reshape(rows, 2 * depth)
    factors = aux_ft.reshape(share, 2 * depth)
    blocks = STEPS * SIDE
    vmem = pl.BlockSpec(memory_space=pltpu.VMEM)
    smem = pl.BlockSpec(memory_space=pltpu.SMEM)
    dma = pltpu.SemaphoreType.DMA
    result = pl.pallas_call(
        kernel,
        out_shape=jax.ShapeDtypeStruct((aux_rows // lax.axis_size("grp"), columns), jnp.bfloat16),
        in_specs=[pl.BlockSpec(memory_space=pl.ANY)] + [vmem] * 4 + [smem] * 5,
        out_specs=vmem,
        scratch_shapes=[
            pltpu.VMEM((STEPS, SIDE, 2, piece, 2 * depth), jnp.bfloat16),
            pltpu.VMEM((blocks, columns, 2 * piece), jnp.float32),
            pltpu.VMEM((blocks, columns, 2 * piece), jnp.bfloat16),
            pltpu.VMEM((blocks, columns, 2 * piece), jnp.bfloat16),
            pltpu.VMEM((blocks, columns, 2 * piece), jnp.bfloat16),
            pltpu.VMEM((blocks, columns, 2 * piece), jnp.bfloat16),
            pltpu.VMEM((columns, 2 * depth), jnp.bfloat16),
            pltpu.VMEM((columns, capacity * rank), jnp.bfloat16),
            pltpu.VMEM((rank, aux_rows), jnp.float32),
            pltpu.VMEM((capacity, aux_rows), jnp.float32),
            pltpu.VMEM((capacity * rank, 2 * share), jnp.bfloat16),
            pltpu.VMEM((4, capacity, 128), jnp.float32),
            dma((HALVES,)),
            dma((blocks * 2,)),
            dma((HALVES * 2,)),
            dma((HALVES,)),
            dma((STEPS * 2,)),
            dma((STEPS,)),
            dma((blocks,)),
            dma((blocks,)),
            dma((blocks,)),
            dma((blocks,)),
            dma((blocks,)),
        ],
        compiler_params=pltpu.CompilerParams(
            collective_id=0, has_side_effects=True, vmem_limit_bytes=60 * 2**20
        ),
    )(
        factors,
        pair_rows,
        aux_basis,
        aux_decay.reshape(aux_rows // 128, 128),
        item_pair,
        image_dist,
        image_phase,
        item_image,
        item_sub,
        item_count,
    )
    return result.reshape(result.shape[0], 2, rows)


def solution(mesh):
    return jax.shard_map(
        body,
        mesh=mesh,
        in_specs=(
            P("dev", None, "grp"),
            P("dev", None, "grp"),
            P("grp"),
            P(),
            P(),
            P(),
            P(),
            P(("grp", "dev"), None, None),
            P(("grp", "dev")),
            P(("grp", "dev")),
            P(("grp", "dev")),
        ),
        out_specs=P("grp", None, "dev"),
        check_vma=False,
    )
```

time: 99.3 us -> 85.3 us (0.86)
  Pallas kernels: 93.4 us -> 79.2 us
    pallas_call x1, Pallas kernels: 93.4 us -> 79.2 us  [body(): pl.pallas_call(kernel, out_shape=jax.ShapeDtypeStruct((aux_rows // lax.ax...]
where the time goes in v2:
time: 85.3 us; the launch traced here: 84.9 us
  Pallas kernels  79.2 us (93%)
  local copies, waits for them, and re-layouts  4.52 us (5%)
    pallas_call x1, Pallas kernels, body(): pl.pallas_call(kernel, out_shape=jax.ShapeDtypeStruct((aux_rows // lax.ax...  79.2 us
    unnamed x6, local copies, waits for them, and re-layouts  2.56 us
    reshape x1, local copies, waits for them, and re-layouts, body(): return result.reshape(result.shape[0], 2, rows)  1.96 us

profile of v2, /device:TPU:32, one launch (start us, length us, event | category | flops | bytes accessed | tf_op | source)
XLA Modules:
  0.0 84.9 jit_solution(17660268396471493725)
XLA Ops:
  0.0 0.0 copy-start
  0.7 0.0 copy-start.1
  0.7 1.7 %copy.12 = bf16[16,8,2,512]{3,1,2,0:T(8,128)(2,1)} copy(bf16[16,8,2,512]{3,2,1,0:T(2,128)(2,1)} %bitcast.8) | data formatting | bytes 524288
  2.4 0.0 copy-done
  2.4 0.0 copy-done.1
  2.4 0.4 multiply_convert_fusion
  2.8 0.9 %copy.13 = bf16[32,8,2,512]{3,1,2,0:T(8,128)(2,1)} copy(bf16[32,8,2,512]{3,2,1,0:T(2,128)(2,1)S(1)} %bitcast.5) | data formatting | bytes 1048576
  3.7 79.2 %shard_map.109 = bf16[512,512]{1,0:T(8,128)(2,1)} custom-call(bf16[128,1024]{1,0:T(8,128)(2,1)} %bitcast.7, bf16[256,1024]{1,0:T(8,128)(2,1)} %bitcast.6, bf16[128,4096]{1,0:T(8,128)(2,1)} %basis_ref.1, f32[32,128]{1,0:T(8,128)} %bitcast.9, bf16[16,128,128]{2,1,0:T(8,128)(2,1)} %items_ref.1, f32[125]{0:T(128)} %dist_ref.1, f32[125]{0:T(128)} %phase_ref.1, ...), custom_call_target="tpu_custom_call" | custom-call | tf_op jit(solution)/shard_map/pallas_call | solution.py:438
  82.9 2.0 %reshape.16 = bf16[512,2,256]{2,1,0:T(2,128)(2,1)} reshape(bf16[512,512]{1,0:T(8,128)(2,1)} %shard_map.109) | data formatting | bytes 1048576 | tf_op jit(solution)/shard_map/reshape | solution.py:483
Async XLA Ops:
  0.0 2.4 %copy-start = (bf16[256,2,512]{2,1,0:T(2,128)(2,1)S(1)}, bf16[256,2,512]{2,1,0:T(2,128)(2,1)}, u32[]{:S(2)}) copy-start(bf16[256,2,512]{2,1,0:T(2,128)(2,1)} %param.11) | copy-start | bytes 1572868
  0.7 1.7 %copy-start.1 = (f32[512]{0:T(512)S(1)}, f32[512]{0:T(512)}, u32[]{:S(2)}) copy-start(f32[512]{0:T(512)} %param.13) | copy-start | bytes 6148

commit v3 on v2

--- a/solution.py
+++ b/solution.py
@@ -15,6 +15,8 @@
 def offset_of(index):
     high = index // 2
     return 2 * high + (high + index) % 2
+DIRECT = 0
+LAGS = (1, 2, 3)
 
 
 def step_of(z_step, half):
@@ -26,11 +28,12 @@
 
 
 def kernel(
-    aux_ref,
-    pair_ref,
-    basis_ref,
+    aux_any,
+    pair_any,
+    basis_any,
+    items_any,
+    weight_ref,
     decay_ref,
-    items_ref,
     dist_ref,
     phase_ref,
     image_ref,
@@ -41,6 +44,7 @@
     total,
     chain_in,
     side_in,
+    far_in,
     pair_in,
     reduce_out,
     long_lhs,
@@ -49,6 +53,10 @@
     damping,
     damped,
     scales,
+    aux_ref,
+    pair_ref,
+    basis_ref,
+    items_ref,
     load_sem,
     factor_recv,
     z_send,
@@ -59,6 +67,7 @@
     reduce_send,
     chain_recv,
     side_recv,
+    far_recv,
     pair_recv,
 ):
     group, member = lax.axis_index("grp"), lax.axis_index("dev")
@@ -70,21 +79,20 @@
     rank = items_ref.shape[1]
     columns = long_lhs.shape[0]
     side_rows = columns // 2
-    depth = pair_ref.shape[1]
-    half_k = depth // 2
+    half_k = pair_ref.shape[2]
+    depth = 2 * half_k
 
     def place(z_at, y_at, core_at):
         return (group, (z_at * 4 + y_at) * 2 + core_at)
 
-    def own_copy(half):
-        return pltpu.make_async_copy(
-            aux_ref.at[pl.ds(half * piece, piece)],
-            factors.at[step_of(0, half), 0, core],
-            load_sem.at[half],
+    loads = [
+        pltpu.make_async_copy(source, sink, load_sem.at[index])
+        for index, (source, sink) in enumerate(
+            ((aux_any, aux_ref), (items_any, items_ref), (basis_any, basis_ref), (pair_any, pair_ref))
         )
-
-    for half in range(HALVES):
-        own_copy(half).start()
+    ]
+    for load in loads:
+        load.start()
 
     sibling = place(z, y, 1 - core)
     z_peers = (place(wrap(z + 1), y, core), place(wrap(z - 1), y, core))
@@ -93,13 +101,19 @@
     y_ahead = place(z, wrap(y + way), core)
     x_down = (z_low * 4 + wrap(x - way), member)
     x_up = (z_low * 4 + wrap(x + way), member)
+    x_far = (z_low * 4 + wrap(x + 2), member)
     z_pair = ((1 - z_low) * 4 + x, member)
     seen_as = (2, 1)
 
-    peers = z_peers + y_peers + (sibling, x_down, x_up, z_pair)
+    peers = z_peers + y_peers + (sibling, x_down, x_up, x_far, z_pair)
     barrier = pltpu.get_barrier_semaphore()
     for peer in peers:
         pl.semaphore_signal(barrier, inc=1, device_id=peer, device_id_type=MESH)
+    loads[0].wait()
+    for half in range(HALVES):
+        own = aux_ref[half * piece : (half + 1) * piece]
+        for part in range(2):
+            factors[step_of(0, half), 0, core, :, part * half_k : (part + 1) * half_k] = own[:, part, :]
     pl.semaphore_wait(barrier, len(peers))
 
     waits = []
@@ -139,7 +153,6 @@
     def send_column(z_step, half):
         step = step_of(z_step, half)
         if z_step == 0:
-            own_copy(half).wait()
             for index, target in enumerate(z_peers):
                 sink = (step_of(seen_as[index], half), 0)
                 send((step, 0), sink, target, z_send.at[half * 2 + index])
@@ -170,9 +183,7 @@
         send((step, 3), (step, 3), sibling, core_send.at[step * 4 + 3])
 
     def prepare():
-        long_lhs[0:side_rows, :] = pair_ref[...]
-        long_lhs[side_rows:columns, 0:half_k] = pair_ref[:, half_k:]
-        long_lhs[side_rows:columns, half_k:] = -pair_ref[:, 0:half_k]
+        loads[1].wait()
 
         slot = lax.broadcasted_iota(jnp.int32, (items, 128), 0)
         phases = jnp.zeros((items, 128), jnp.float32)
@@ -203,6 +214,8 @@
 
         lax.fori_loop(0, items, place_item, 0)
 
+        loads[2].wait()
+
         def by_halves(left, right):
             low = lax.broadcasted_iota(jnp.int32, left.shape, 1) < piece
             return (
@@ -223,6 +236,22 @@
             return carry
 
         lax.fori_loop(0, basis_cols.shape[1] // 256, arrange, 0)
+
+    def weigh():
+        loads[3].wait()
+
+        def rows_of(index, carry):
+            at = pl.ds(pl.multiple_of(index * 32, 32), 32)
+            low = pl.ds(pl.multiple_of(side_rows + index * 32, 32), 32)
+            scaled = (pair_ref[at].astype(jnp.float32) * weight_ref[...][None]).astype(jnp.bfloat16)
+            real_part, imag_part = scaled[:, 0, :], scaled[:, 1, :]
+            long_lhs[at, 0:half_k] = real_part
+            long_lhs[at, half_k:] = imag_part
+            long_lhs[low, 0:half_k] = imag_part
+            long_lhs[low, half_k:] = -real_part
+            return carry
+
+        lax.fori_loop(0, side_rows // 32, rows_of, 0)
 
     def short_range(z_step):
         def one(y_step, carry):
@@ -261,6 +290,9 @@
 
     def side_copy(block):
         return reduce_copy(block, side_in, side_recv, x_up)
+
+    def far_copy(block):
+        return reduce_copy(block, far_in, far_recv, x_far)
 
     def pair_copy(block):
         return reduce_copy(block, pair_in, pair_recv, z_pair)
@@ -282,13 +314,21 @@
                 total[block] += product[:, row * 128 : (row + 1) * 128]
                 role, _, _ = roles(z_step, first_row + row)
 
-                @pl.when(role >= 2)
+                direct = quad in QUADS[len(QUADS) - DIRECT :]
+
+                @pl.when(role >= (1 if direct else 2))
                 def _():
                     reduce_out[block] = total[block].astype(jnp.bfloat16)
 
-                @pl.when(role == 2)
+                @pl.when(role == (1 if direct else 2))
                 def _():
                     chain_copy(block).start()
+
+                if direct:
+
+                    @pl.when(role == 2)
+                    def _():
+                        far_copy(block).start()
 
                 @pl.when(role == 3)
                 def _():
@@ -300,6 +340,9 @@
 
     def reduce_hop(quad, hop):
         first_z, first_row, half = quad
+        direct = quad in QUADS[len(QUADS) - DIRECT :]
+        if direct and hop == 1:
+            return
 
         def one(index, carry):
             z_step = first_z + index // 2
@@ -322,9 +365,11 @@
                 def _():
                     side_copy(block).wait_recv()
                     chain_copy(block).wait_recv()
-                    total[block] += chain_in[block].astype(jnp.float32) + side_in[block].astype(
-                        jnp.float32
-                    )
+                    others = chain_in[block].astype(jnp.float32) + side_in[block].astype(jnp.float32)
+                    if direct:
+                        far_copy(block).wait_recv()
+                        others += far_in[block].astype(jnp.float32)
+                    total[block] += others
 
                 @pl.when((role == 0) & jnp.logical_not(keeps))
                 def _():
@@ -350,9 +395,9 @@
     def advance(index):
         if index < len(QUADS):
             long_range(QUADS[index])
-        for hop in (1, 2, 3):
-            if 0 <= index - hop < len(QUADS):
-                reduce_hop(QUADS[index - hop], hop)
+        for hop, lag in zip((1, 2, 3), LAGS):
+            if 0 <= index - lag < len(QUADS):
+                reduce_hop(QUADS[index - lag], hop)
 
     send_column(0, 0)
     send_column(0, 1)
@@ -362,6 +407,7 @@
     send_rows(0, 1)
     send_column(1, 0)
     send_column(2, 0)
+    weigh()
     short_range(1)
     send_far(0, 0)
     send_rows(1, 0)
@@ -390,23 +436,25 @@
     send_far(2, 1)
     advance(6)
     send_far(3, 1)
-    for index in range(7, 11):
-        advance(index)
-
+    def drain(block, carry):
+        role, keeps, _ = roles(block // (HALVES * SIDE), block % SIDE)
+
+        @pl.when((role > 0) | jnp.logical_not(keeps))
+        def _():
+            chain_copy(block).wait_send()
+
+        return carry
+
+    advance(7)
     for copy in waits:
         copy.wait_send()
     for half in range(HALVES):
         relay_copy(1, half).wait_send()
-    def drain(block, carry):
-        role, keeps, _ = roles(block // (HALVES * SIDE), block % SIDE)
-
-        @pl.when((role > 0) | jnp.logical_not(keeps))
-        def _():
-            chain_copy(block).wait_send()
-
-        return carry
-
-    lax.fori_loop(0, STEPS * SIDE, drain, 0)
+    for index in range(8, len(QUADS) + LAGS[2]):
+        advance(index)
+        if index == 8:
+            lax.fori_loop(0, STEPS * SIDE // 2, drain, 0)
+    lax.fori_loop(STEPS * SIDE // 2, STEPS * SIDE, drain, 0)
 
 
 def body(
@@ -428,9 +476,6 @@
     capacity, rank, _ = item_pair.shape
     columns = 2 * rows
     piece = share // HALVES
-    weighted = (pair_ft.astype(jnp.float32) * coul_weight[None, None, :]).astype(jnp.bfloat16)
-    pair_rows = weighted.reshape(rows, 2 * depth)
-    factors = aux_ft.reshape(share, 2 * depth)
     blocks = STEPS * SIDE
     vmem = pl.BlockSpec(memory_space=pltpu.VMEM)
     smem = pl.BlockSpec(memory_space=pltpu.SMEM)
@@ -438,11 +483,12 @@
     result = pl.pallas_call(
         kernel,
         out_shape=jax.ShapeDtypeStruct((aux_rows // lax.axis_size("grp"), columns), jnp.bfloat16),
-        in_specs=[pl.BlockSpec(memory_space=pl.ANY)] + [vmem] * 4 + [smem] * 5,
+        in_specs=[pl.BlockSpec(memory_space=pl.ANY)] * 4 + [vmem] * 2 + [smem] * 5,
         out_specs=vmem,
         scratch_shapes=[
             pltpu.VMEM((STEPS, SIDE, 2, piece, 2 * depth), jnp.bfloat16),
             pltpu.VMEM((blocks, columns, 2 * piece), jnp.float32),
+            pltpu.VMEM((blocks, columns, 2 * piece), jnp.bfloat16),
             pltpu.VMEM((blocks, columns, 2 * piece), jnp.bfloat16),
             pltpu.VMEM((blocks, columns, 2 * piece), jnp.bfloat16),
             pltpu.VMEM((blocks, columns, 2 * piece), jnp.bfloat16),
@@ -453,7 +499,11 @@
             pltpu.VMEM((capacity, aux_rows), jnp.float32),
             pltpu.VMEM((capacity * rank, 2 * share), jnp.bfloat16),
             pltpu.VMEM((4, capacity, 128), jnp.float32),
-            dma((HALVES,)),
+            pltpu.VMEM((share, 2, depth), jnp.bfloat16),
+            pltpu.VMEM((rows, 2, depth), jnp.bfloat16),
+            pltpu.VMEM((rank, aux_rows), jnp.bfloat16),
+            pltpu.VMEM((capacity, rank, 128), jnp.bfloat16),
+            dma((4,)),
             dma((blocks * 2,)),
             dma((HALVES * 2,)),
             dma((HALVES,)),
@@ -464,16 +514,18 @@
             dma((blocks,)),
             dma((blocks,)),
             dma((blocks,)),
+            dma((blocks,)),
         ],
         compiler_params=pltpu.CompilerParams(
             collective_id=0, has_side_effects=True, vmem_limit_bytes=60 * 2**20
         ),
     )(
-        factors,
-        pair_rows,
+        aux_ft,
+        pair_ft,
         aux_basis,
+        item_pair,
+        coul_weight.reshape(1, depth),
         aux_decay.reshape(aux_rows // 128, 128),
-        item_pair,
         image_dist,
         image_phase,
         item_image,

time: 85.3 us -> 81.5 us (0.955)
  local copies, waits for them, and re-layouts: 4.52 us -> 1.96 us
    unnamed x6 -> x0, local copies, waits for them, and re-layouts: 2.56 us -> none
    pallas_call x1, Pallas kernels: 79.2 us -> 78.4 us  [body(): pl.pallas_call(kernel, out_shape=jax.ShapeDtypeStruct((aux_rows // lax.ax...]
where the time goes in v3:
time: 81.5 us; the launch traced here: 81 us
  Pallas kernels  78.4 us (96%)
  local copies, waits for them, and re-layouts  1.96 us (2%)
    pallas_call x1, Pallas kernels, body(): pl.pallas_call(kernel, out_shape=jax.ShapeDtypeStruct((aux_rows // lax.ax...  78.4 us
    reshape x1, local copies, waits for them, and re-layouts, body(): return result.reshape(result.shape[0], 2, rows)  1.96 us

profile of v3, /device:TPU:32, one launch (start us, length us, event | category | flops | bytes accessed | tf_op | source)
XLA Modules:
  0.0 81.0 jit_solution(1546346349454400825)
XLA Ops:
  0.7 78.4 %shard_map.109 = bf16[512,512]{1,0:T(8,128)(2,1)} custom-call(bf16[128,2,512]{2,1,0:T(2,128)(2,1)} %aux_any.1, bf16[256,2,512]{2,1,0:T(2,128)(2,1)} %pair_any.1, bf16[128,4096]{1,0:T(8,128)(2,1)} %basis_any.1, bf16[16,128,128]{2,1,0:T(8,128)(2,1)} %items_any.1, f32[1,512]{1,0:T(1,128)} %bitcast.3, f32[32,128]{1,0:T(8,128)} %bitcast.2, f32[125]{0:T(128)} %dist_ref.1, ...), custom_call_target="tpu_custom_call" | custom-call | tf_op jit(solution)/shard_map/pallas_call | solution.py:483
  79.0 2.0 %reshape.11 = bf16[512,2,256]{2,1,0:T(2,128)(2,1)} reshape(bf16[512,512]{1,0:T(8,128)(2,1)} %shard_map.109) | data formatting | bytes 1048576 | tf_op jit(solution)/shard_map/reshape | solution.py:535

commit v4 on v3

--- a/solution.py
+++ b/solution.py
@@ -16,7 +16,7 @@
     high = index // 2
     return 2 * high + (high + index) % 2
 DIRECT = 0
-LAGS = (1, 2, 3)
+LAGS = (1, 3, 4)
 
 
 def step_of(z_step, half):
@@ -393,11 +393,16 @@
         lax.fori_loop(0, SIDE, one, 0)
 
     def advance(index):
+        def hop_of(hop):
+            at = index - LAGS[hop - 1]
+            if 0 <= at < len(QUADS):
+                reduce_hop(QUADS[at], hop)
+
+        hop_of(2)
+        hop_of(3)
         if index < len(QUADS):
             long_range(QUADS[index])
-        for hop, lag in zip((1, 2, 3), LAGS):
-            if 0 <= index - lag < len(QUADS):
-                reduce_hop(QUADS[index - lag], hop)
+        hop_of(1)
 
     send_column(0, 0)
     send_column(0, 1)
@@ -413,13 +418,13 @@
     send_rows(1, 0)
     send_far(0, 1)
     send_column(1, 1)
+    short_range(2)
     advance(0)
     send_rows(2, 0)
     send_far(1, 0)
     send_column(3, 0)
     send_column(2, 1)
     advance(1)
-    short_range(2)
     send_rows(1, 1)
     send_column(3, 1)
     advance(2)
@@ -431,8 +436,8 @@
     send_rows(2, 1)
     advance(4)
     send_far(3, 0)
+    advance(5)
     send_rows(3, 1)
-    advance(5)
     send_far(2, 1)
     advance(6)
     send_far(3, 1)

time: 81.5 us -> 80.6 us (0.989)
  no operation moved by 1% of the time
where the time goes in v4:
time: 80.6 us; the launch traced here: 80.4 us
  Pallas kernels  77.8 us (97%)
  local copies, waits for them, and re-layouts  1.96 us (2%)
    pallas_call x1, Pallas kernels, body(): pl.pallas_call(kernel, out_shape=jax.ShapeDtypeStruct((aux_rows // lax.ax...  77.8 us
    reshape x1, local copies, waits for them, and re-layouts, body(): return result.reshape(result.shape[0], 2, rows)  1.96 us

profile of v4, /device:TPU:32, one launch (start us, length us, event | category | flops | bytes accessed | tf_op | source)
XLA Modules:
  0.0 80.4 jit_solution(13584705266955091160)
XLA Ops:
  0.7 77.8 %shard_map.109 = bf16[512,512]{1,0:T(8,128)(2,1)} custom-call(bf16[128,2,512]{2,1,0:T(2,128)(2,1)} %aux_any.1, bf16[256,2,512]{2,1,0:T(2,128)(2,1)} %pair_any.1, bf16[128,4096]{1,0:T(8,128)(2,1)} %basis_any.1, bf16[16,128,128]{2,1,0:T(8,128)(2,1)} %items_any.1, f32[1,512]{1,0:T(1,128)} %bitcast.3, f32[32,128]{1,0:T(8,128)} %bitcast.2, f32[125]{0:T(128)} %dist_ref.1, ...), custom_call_target="tpu_custom_call" | custom-call | tf_op jit(solution)/shard_map/pallas_call | solution.py:488
  78.4 2.0 %reshape.11 = bf16[512,2,256]{2,1,0:T(2,128)(2,1)} reshape(bf16[512,512]{1,0:T(8,128)(2,1)} %shard_map.109) | data formatting | bytes 1048576 | tf_op jit(solution)/shard_map/reshape | solution.py:540

commit v5 on v4

--- a/solution.py
+++ b/solution.py
@@ -105,7 +105,7 @@
     z_pair = ((1 - z_low) * 4 + x, member)
     seen_as = (2, 1)
 
-    peers = z_peers + y_peers + (sibling, x_down, x_up, x_far, z_pair)
+    peers = z_peers + y_peers + (sibling, x_down, x_up, z_pair)
     barrier = pltpu.get_barrier_semaphore()
     for peer in peers:
         pl.semaphore_signal(barrier, inc=1, device_id=peer, device_id_type=MESH)
@@ -425,6 +425,7 @@
     send_column(3, 0)
     send_column(2, 1)
     advance(1)
+    short_range(3)
     send_rows(1, 1)
     send_column(3, 1)
     advance(2)
@@ -432,7 +433,6 @@
     send_far(1, 1)
     send_rows(3, 0)
     advance(3)
-    short_range(3)
     send_rows(2, 1)
     advance(4)
     send_far(3, 0)

time: 80.6 us -> 79.9 us (level)
  Pallas kernels: 77.8 us -> 76.9 us
    pallas_call x1, Pallas kernels: 77.8 us -> 76.9 us  [body(): pl.pallas_call(kernel, out_shape=jax.ShapeDtypeStruct((aux_rows // lax.ax...]
where the time goes in v5:
time: 79.9 us; the launch traced here: 79.6 us
  Pallas kernels  76.9 us (96%)
  local copies, waits for them, and re-layouts  1.96 us (2%)
    pallas_call x1, Pallas kernels, body(): pl.pallas_call(kernel, out_shape=jax.ShapeDtypeStruct((aux_rows // lax.ax...  76.9 us
    reshape x1, local copies, waits for them, and re-layouts, body(): return result.reshape(result.shape[0], 2, rows)  1.96 us

profile of v5, /device:TPU:32, one launch (start us, length us, event | category | flops | bytes accessed | tf_op | source)
XLA Modules:
  0.0 79.6 jit_solution(6165891971916145170)
XLA Ops:
  0.7 76.9 %shard_map.109 = bf16[512,512]{1,0:T(8,128)(2,1)} custom-call(bf16[128,2,512]{2,1,0:T(2,128)(2,1)} %aux_any.1, bf16[256,2,512]{2,1,0:T(2,128)(2,1)} %pair_any.1, bf16[128,4096]{1,0:T(8,128)(2,1)} %basis_any.1, bf16[16,128,128]{2,1,0:T(8,128)(2,1)} %items_any.1, f32[1,512]{1,0:T(1,128)} %bitcast.3, f32[32,128]{1,0:T(8,128)} %bitcast.2, f32[125]{0:T(128)} %dist_ref.1, ...), custom_call_target="tpu_custom_call" | custom-call | tf_op jit(solution)/shard_map/pallas_call | solution.py:488
  77.6 2.0 %reshape.11 = bf16[512,2,256]{2,1,0:T(2,128)(2,1)} reshape(bf16[512,512]{1,0:T(8,128)(2,1)} %shard_map.109) | data formatting | bytes 1048576 | tf_op jit(solution)/shard_map/reshape | solution.py:540
